TPU v7x, 32 devices: a whole 2x2x4 slice. The times are simulated.
32 devices in a mesh: group: 2 (over y), tm: 4 (over z), mp: 4 (over x, core).
Axes of the slice: x: 2, y: 2, z: 4, core: 2. Of those that a mesh axis runs over, the one named last changes fastest.
Arguments:
- latents: bfloat16 [2, 4, 256, 1536], P('group', 'tm'), parts along dimension 0, may hold values from -6 to 6
- gsd_table: float32 [8, 6, 1536], replicated, may hold values from -3 to 3
- gsd_bucket: int32 [2, 4], P('group', 'tm'), parts along dimension 0, may hold values from 0 to 7
- clearest: int32 [2], P('group'), parts along dimension 0, may hold values from 0 to 3, as said below
- clouds: int32 [2, 4, 256], P('group'), parts along dimension 0, may hold values from 0 to 1
- cross_query: bfloat16 [1536, 1536], P('tm', 'mp'), may hold values from -5 to 5
- cross_pairs: bfloat16 [1536, 2, 1536], P('tm', None, 'mp'), may hold values from -5 to 5
- cross_merge: bfloat16 [1536, 1536], P('mp', 'tm'), may hold values from -0.15625 to 0.15625
- time_triple: bfloat16 [1536, 3, 1536], P('tm', None, 'mp'), may hold values from -5 to 5
- time_merge: bfloat16 [1536, 1536], P('mp', 'tm'), may hold values from -0.15625 to 0.15625
Outputs:
- updated: bfloat16 [2, 4, 256, 1536], P('group', 'tm'), parts along dimension 0
There are 2 independent parts, one for each index of `group`. A program takes and returns all parts, laid end to end along the dimension named above; an argument that names none is the same for every part. Nothing has to cross between parts.
Inputs may be any that keep to these rules, and one draw needn't show every extreme that they name: clearest[s] is one of the stack's dates; that date has no cloudy token, and no date of stack s has fewer cloudy tokens.
All inputs are finite; a program needn't handle non-finite values.
Results may differ from a plain program's by a relative error of at most 0.014.
The roundings to bfloat16 on the way count: a program that leaves them out, or rounds other values in their place, can miss the bound.
Values may be sent and summed in bfloat16 or wider, within the bound.
A program may use at most 64 MiB of HBM per device.

v0:
```python
import jax
import jax.numpy as jnp
from jax import lax
from jax.sharding import PartitionSpec as P

HEAD_DIM = 64


def broadcast(block, axis, holder):
    block = jnp.where(lax.axis_index(axis) == holder, block, jnp.zeros_like(block))
    return lax.psum(block, axis)


def normalize(values):
    centre = jnp.mean(values, axis=-1, keepdims=True)
    shifted = values - centre
    variance = jnp.mean(shifted * shifted, axis=-1, keepdims=True)
    return shifted * lax.rsqrt(variance + 1e-06)


def softmax_rows(scores):
    highest = jnp.max(scores, axis=-1, keepdims=True)
    weights = jnp.exp(scores - highest)
    return weights / jnp.sum(weights, axis=-1, keepdims=True)


def shards(
    latents,
    gsd_table,
    gsd_bucket,
    clearest,
    clouds,
    cross_query,
    cross_pairs,
    cross_merge,
    time_triple,
    time_merge,
):
    stacks = latents.shape[0]
    seq_tokens = latents.shape[2]
    model_width = latents.shape[3]
    local_width = cross_query.shape[1]
    local_heads = local_width // HEAD_DIM
    buckets = gsd_table.shape[0]
    scale_factor = HEAD_DIM ** (-0.5)
    my_buckets = gsd_bucket.reshape(stacks)
    one_hot = (my_buckets[:, None] == jnp.arange(buckets, dtype=jnp.int32)[None, :]).astype(
        jnp.float32
    )
    modulation = jnp.dot(
        one_hot, gsd_table.reshape(buckets, 6 * model_width), precision=lax.Precision.HIGHEST
    ).reshape(stacks, 6, 1, 1, model_width)
    values = latents.astype(jnp.float32)
    normed = (normalize(values) * (1.0 + modulation[:, 1]) + modulation[:, 0]).astype(jnp.bfloat16)
    full_query, full_pairs, full_merge, full_triple, full_time = (
        lax.all_gather(cross_query, "tm", axis=0, tiled=True),
        lax.all_gather(cross_pairs, "tm", axis=0, tiled=True),
        lax.all_gather(cross_merge, "tm", axis=1, tiled=True),
        lax.all_gather(time_triple, "tm", axis=0, tiled=True),
        lax.all_gather(time_merge, "tm", axis=1, tiled=True),
    )
    flat_rows = normed.reshape(stacks * seq_tokens, model_width)
    queries = jnp.dot(flat_rows, full_query, preferred_element_type=jnp.float32).astype(
        jnp.bfloat16
    )

    def project_reference(ref_rows):
        return jnp.einsum(
            "ld,dce->lce", ref_rows, full_pairs, preferred_element_type=jnp.float32
        ).astype(jnp.bfloat16)

    def empty_pairs(ref_rows):
        return jnp.zeros((ref_rows.shape[0], 2, local_width), jnp.bfloat16)

    position = lax.axis_index("tm")
    owner_date = clearest[0]
    local_pair = lax.cond(position == owner_date, project_reference, empty_pairs, normed[0, 0])
    key_pair = broadcast(local_pair, "tm", owner_date)
    pair_list = [key_pair]
    key_pairs = jnp.stack(pair_list)
    heads_query = queries.reshape(stacks, seq_tokens, local_heads, HEAD_DIM)
    heads_key = key_pairs[:, :, 0].reshape(stacks, seq_tokens, local_heads, HEAD_DIM)
    heads_value = key_pairs[:, :, 1].reshape(stacks, seq_tokens, local_heads, HEAD_DIM)
    scores = (
        jnp.einsum("sqhe,skhe->shqk", heads_query, heads_key, preferred_element_type=jnp.float32)
        * scale_factor
    )
    attn_weights = softmax_rows(scores).astype(jnp.bfloat16)
    attended = jnp.einsum(
        "shqk,skhe->sqhe", attn_weights, heads_value, preferred_element_type=jnp.float32
    ).astype(jnp.bfloat16)
    cross_terms = jnp.dot(
        attended.reshape(stacks * seq_tokens, local_width),
        full_merge,
        preferred_element_type=jnp.float32,
    )
    cross_sum = lax.psum(cross_terms.astype(jnp.bfloat16), "mp").astype(jnp.float32)
    middle = values + modulation[:, 2] * cross_sum.reshape(stacks, 1, seq_tokens, model_width)
    normed_two = (normalize(middle) * (1.0 + modulation[:, 4]) + modulation[:, 3]).astype(
        jnp.bfloat16
    )
    triple = jnp.einsum(
        "nd,dce->nce",
        normed_two.reshape(stacks * seq_tokens, model_width),
        full_triple,
        preferred_element_type=jnp.float32,
    ).astype(jnp.bfloat16)
    triple = triple.reshape(stacks, 1, seq_tokens, 3, local_width)
    patches = lax.all_to_all(triple, "tm", split_axis=2, concat_axis=1, tiled=True)
    date_count = patches.shape[1]
    patch_count = patches.shape[2]
    allowed = lax.dynamic_slice_in_dim(clouds == 0, position * patch_count, patch_count, 2)
    split_heads = patches.reshape(stacks, date_count, patch_count, 3, local_heads, HEAD_DIM)
    scores_time = (
        jnp.einsum(
            "sdphe,sfphe->sphdf",
            split_heads[:, :, :, 0],
            split_heads[:, :, :, 1],
            preferred_element_type=jnp.float32,
        )
        * scale_factor
    )
    visible = jnp.transpose(allowed, (0, 2, 1))[:, :, None, None, :]
    scores_time = jnp.where(visible, scores_time, -1e30)
    time_weights = softmax_rows(scores_time).astype(jnp.bfloat16)
    mixed_out = jnp.einsum(
        "sphdf,sfphe->sdphe",
        time_weights,
        split_heads[:, :, :, 2],
        preferred_element_type=jnp.float32,
    ).astype(jnp.bfloat16)
    mixed_out = mixed_out.reshape(stacks, date_count, patch_count, local_width)
    returned = lax.all_to_all(mixed_out, "tm", split_axis=1, concat_axis=2, tiled=True)
    time_terms = jnp.dot(
        returned.reshape(stacks * seq_tokens, local_width),
        full_time,
        preferred_element_type=jnp.float32,
    )
    time_sum = lax.psum(time_terms.astype(jnp.bfloat16), "mp").astype(jnp.float32)
    return (
        middle + modulation[:, 5] * time_sum.reshape(stacks, 1, seq_tokens, model_width)
    ).astype(jnp.bfloat16)


def solution(mesh):
    placed = (
        P("group", "tm", None, None),
        P(),
        P("group", "tm"),
        P("group"),
        P("group", None, None),
        P("tm", "mp"),
        P("tm", None, "mp"),
        P("mp", "tm"),
        P("tm", None, "mp"),
        P("mp", "tm"),
    )
    return jax.shard_map(
        shards, mesh=mesh, in_specs=placed, out_specs=P("group", "tm", None, None), check_vma=False
    )
```

profile of v0, /device:TPU:0, one launch (start us, length us, event | category | flops | bytes accessed | tf_op | source)
XLA Modules:
  0.0 375.0 jit_solution(14642475833497510122)
XLA Ops:
  6.5 2.0 copy.47
  8.7 0.7 all-gather.8.cloned.1.call-update
  10.1 0.3 fusion.26
  11.0 0.1 slice_reduce_fusion.1
  11.1 0.2 convert_reduce_fusion
  11.3 0.3 fusion.6
  11.7 0.4 fusion.19
  12.1 50.1 %all-gather.6.cloned.1.call-done = bf16[1536,2,384]{2,0,1:T(8,128)(2,1)} async-done(((bf16[384,2,384]{2,0,1:T(8,128)(2,1)}), bf16[1536,2,384]{2,0,1:T(8,128)(2,1)}) %all-gather.6.cloned.1.call-update) | async-done | bytes 2359312 | tf_op jit(solution)/shard_map/all_gather | solution.py:57
  62.2 0.8 select_bitcast_fusion
  63.1 0.5 all-gather.10.cloned.1.call-update
  63.7 29.4 %all-gather.8.cloned.1.call-done = bf16[1536,384]{1,0:T(8,128)(2,1)} async-done(((bf16[384,384]{1,0:T(8,128)(2,1)}), bf16[1536,384]{1,0:T(8,128)(2,1)}) %all-gather.8.cloned.1.call-update) | async-done | bytes 1179664 | tf_op jit(solution)/shard_map/all_gather | solution.py:56
  93.0 1.8 convolution_convert_fusion.5
  94.9 0.1 copy.49
  95.0 36.6 %all-reduce.4.cloned.1.call-done = bf16[1,256,2,384]{3,1,2,0:T(8,128)(2,1)} async-done(((bf16[1,256,2,384]{3,1,2,0:T(8,128)(2,1)}), bf16[1,256,2,384]{3,1,2,0:T(8,128)(2,1)}) %all-reduce.4.cloned.1.call-update) | async-done | bytes 393232 | tf_op jit(solution)/shard_map/psum | solution.py:11
  131.6 1.1 fusion.44
  132.7 0.1 copy.50
  132.8 0.1 copy.48
  133.0 0.7 fusion.45
  133.6 0.3 convolution_convert_fusion.6
  133.9 29.0 %all-gather.10.cloned.1.call-done = bf16[384,1536]{1,0:T(8,128)(2,1)} async-done(((bf16[384,384]{1,0:T(8,128)(2,1)}), bf16[384,1536]{1,0:T(8,128)(2,1)}) %all-gather.10.cloned.1.call-update) | async-done | bytes 1179664 | tf_op jit(solution)/shard_map/all_gather | solution.py:58
  162.9 2.7 convolution_convert_fusion.2
  165.7 0.0 all-gather.12.cloned.1.call-start
  165.7 0.5 all-gather.12.cloned.1.call-update
  166.2 33.6 %all-reduce.6.cloned.1.call-done = bf16[256,1536]{1,0:T(8,128)(2,1)} async-done(((bf16[256,1536]{1,0:T(8,128)(2,1)}), bf16[256,1536]{1,0:T(8,128)(2,1)}) %all-reduce.6.cloned.1.call-update) | async-done | bytes 786448 | tf_op jit(solution)/shard_map/psum | solution.py:97
  199.9 1.5 fusion.16
  201.4 0.4 multiply_reduce_fusion
  201.9 69.5 %all-gather.12.cloned.1.call-done = bf16[1536,3,384]{2,0,1:T(8,128)(2,1)} async-done(((bf16[384,3,384]{2,0,1:T(8,128)(2,1)}), bf16[1536,3,384]{2,0,1:T(8,128)(2,1)}) %all-gather.12.cloned.1.call-update) | async-done | bytes 3538960 | tf_op jit(solution)/shard_map/all_gather | solution.py:59
  271.4 3.2 fusion.12
  274.7 1.4 copy.52
  276.1 4.2 %all-to-all-start = ((bf16[1,1,256,3,384]{4,3,1,0,2:T(4,128)(2,1)}), bf16[1,1,256,3,384]{4,3,1,0,2:T(4,128)(2,1)}, u32[]{:S(2)}, u32[]{:S(2)}) async-start(bf16[1,1,256,3,384]{4,3,1,0,2:T(4,128)(2,1)} %copy.52), calls=%async_computation | async-start | bytes 1572864 | tf_op jit(solution)/shard_map/all_to_all | solution.py:109
  280.3 0.7 all-gather.14.cloned.1.call-update
  281.0 0.1 fusion.34
  281.1 31.1 %all-to-all-done = bf16[1,1,256,3,384]{4,3,1,0,2:T(4,128)(2,1)} async-done(((bf16[1,1,256,3,384]{4,3,1,0,2:T(4,128)(2,1)}), bf16[1,1,256,3,384]{4,3,1,0,2:T(4,128)(2,1)}, u32[]{:S(2)}, u32[]{:S(2)}) %all-to-all-start) | async-done | bytes 589856 | tf_op jit(solution)/shard_map/all_to_all | solution.py:109
  312.2 2.7 reshape.227
  315.0 1.1 fusion.43
  316.0 0.6 fusion.25
  316.6 0.3 copy.57
  317.0 0.1 fusion.46
  317.1 0.3 copy.58
  317.4 0.6 fusion.13
  318.0 0.1 copy.59
  318.1 1.0 reshape.221
  319.1 3.4 all-to-all-start.1
  322.5 0.0 all-reduce.8.cloned.1.call-start
  322.5 6.1 %all-to-all-done.1 = bf16[1,4,64,384]{3,2,0,1:T(8,128)(2,1)S(1)} async-done(((bf16[1,4,64,384]{3,2,0,1:T(8,128)(2,1)}), bf16[1,4,64,384]{3,2,0,1:T(8,128)(2,1)S(1)}, u32[]{:S(2)}, u32[]{:S(2)}) %all-to-all-start.1) | async-done | bytes 196640 | tf_op jit(solution)/shard_map/all_to_all | solution.py:133
  328.7 2.7 convolution_convert_fusion.1
  331.4 34.3 %all-reduce.8.cloned.1.call-done = bf16[256,1536]{1,0:T(8,128)(2,1)} async-done(((bf16[256,1536]{1,0:T(8,128)(2,1)}), bf16[256,1536]{1,0:T(8,128)(2,1)}) %all-reduce.8.cloned.1.call-update) | async-done | bytes 786448 | tf_op jit(solution)/shard_map/psum | solution.py:139
  365.8 2.4 fusion.10
  (29 shorter events, 0.4 us)
Async XLA Ops:
  6.5 3.5 copy-start
  6.5 4.6 %copy-start.1 = (bf16[1,1,256,1536]{3,2,1,0:T(8,128)(2,1)S(1)}, bf16[1,1,256,1536]{3,2,1,0:T(8,128)(2,1)}, u32[]{:S(2)}) copy-start(bf16[1,1,256,1536]{3,2,1,0:T(8,128)(2,1)} %param.12) | copy-start | bytes 2359300
  6.5 55.6 %all-gather.6.cloned.1.call-start = ((), (), s32[]{:S(2)}) async-start(), calls=%async_computation.2 | async-start | bytes 2949120 | tf_op jit(solution)/shard_map/all_gather | solution.py:57
  8.6 84.4 %all-gather.8.cloned.1.call-start = ((), (), s32[]{:S(2)}) async-start(), calls=%async_computation.4 | async-start | bytes 1474560 | tf_op jit(solution)/shard_map/all_gather | solution.py:56
  9.4 122.2 %all-reduce.4.cloned.1.call-start = ((), (), s32[]{:S(2)}) async-start(), calls=%async_computation.3 | async-start | bytes 786432 | tf_op jit(solution)/shard_map/psum | solution.py:11
  63.0 99.8 %all-gather.10.cloned.1.call-start = ((), (), s32[]{:S(2)}) async-start(), calls=%async_computation.5 | async-start | bytes 1474560 | tf_op jit(solution)/shard_map/all_gather | solution.py:58
  63.6 136.3 %all-reduce.6.cloned.1.call-start = ((), (), s32[]{:S(2)}) async-start(), calls=%async_computation.6 | async-start | bytes 1572864 | tf_op jit(solution)/shard_map/psum | solution.py:97
  165.7 105.8 %all-gather.12.cloned.1.call-start = ((), (), s32[]{:S(2)}) async-start(), calls=%async_computation.7 | async-start | bytes 4423680 | tf_op jit(solution)/shard_map/all_gather | solution.py:59
  199.9 1.6 copy-start.2
  274.7 6.4 %copy-start.4 = (s32[1,4,256]{2,1,0:T(4,128)S(1)}, s32[1,4,256]{2,1,0:T(4,128)}, u32[]{:S(2)}) copy-start(s32[1,4,256]{2,1,0:T(4,128)} %param.16) | copy-start | bytes 12292
  276.1 36.2 %all-to-all-start = ((bf16[1,1,256,3,384]{4,3,1,0,2:T(4,128)(2,1)}), bf16[1,1,256,3,384]{4,3,1,0,2:T(4,128)(2,1)}, u32[]{:S(2)}, u32[]{:S(2)}) async-start(bf16[1,1,256,3,384]{4,3,1,0,2:T(4,128)(2,1)} %copy.52), calls=%async_computation | async-start | bytes 1572864 | tf_op jit(solution)/shard_map/all_to_all | solution.py:109
  280.3 42.3 %all-gather.14.cloned.1.call-start = ((), (), s32[]{:S(2)}) async-start(), calls=%async_computation.8 | async-start | bytes 1474560 | tf_op jit(solution)/shard_map/all_gather | solution.py:60
  316.0 1.4 copy-start.3
  319.1 9.6 %all-to-all-start.1 = ((bf16[1,4,64,384]{3,2,0,1:T(8,128)(2,1)}), bf16[1,4,64,384]{3,2,0,1:T(8,128)(2,1)S(1)}, u32[]{:S(2)}, u32[]{:S(2)}) async-start(bf16[1,4,64,384]{3,2,0,1:T(8,128)(2,1)} %bitcast.30), calls=%async_computation.1 | async-start | bytes 393216 | tf_op jit(solution)/shard_map/all_to_all | solution.py:133
  322.5 43.3 %all-reduce.8.cloned.1.call-start = ((), (), s32[]{:S(2)}) async-start(), calls=%async_computation.9 | async-start | bytes 1572864 | tf_op jit(solution)/shard_map/psum | solution.py:139
Sparse Core Ops, SparseCore 0:
  8.9 53.2 all-gather.5
  63.7 29.2 all-gather.7
  95.4 36.1 all-reduce.3
  133.1 29.7 all-gather.9
  165.8 34.0 all-reduce.5
  201.4 69.9 all-gather.11
  282.8 37.2 all-gather.13
  331.6 34.1 all-reduce.7
where the time goes:
time: 376 us; the launch traced here: 375 us
  waiting for transfers between devices  322 us (86%)
  between operations  15 us (4%)
  matrix products  12.9 us (3%)
  local copies, waits for them, and re-layouts  10.5 us (3%)
  starting transfers between devices  7.84 us (2%)
  other arithmetic  6.42 us (2%)
    all_gather x1, waiting for transfers between devices, shards(): lax.all_gather(time_triple, 'tm', axis=0, tiled=True)  69.5 us
    all_gather x1, waiting for transfers between devices, shards(): lax.all_gather(cross_pairs, 'tm', axis=0, tiled=True)  50.1 us
    psum x1, waiting for transfers between devices, broadcast(): return lax.psum(block, axis)  36.6 us
    psum x1, waiting for transfers between devices, shards(): lax.psum(time_terms.astype(jnp.bfloat16), 'mp').astype(jnp.float32)  34.3 us
    psum x1, waiting for transfers between devices, shards(): lax.psum(cross_terms.astype(jnp.bfloat16), 'mp').astype(jnp.float32)  33.6 us
    all_to_all x1, waiting for transfers between devices, shards(): lax.all_to_all(triple, 'tm', split_axis=2, concat_axis=1, tiled=True)  31.1 us
    all_gather x1, waiting for transfers between devices, shards(): lax.all_gather(cross_query, 'tm', axis=0, tiled=True)  29.4 us
    all_gather x1, waiting for transfers between devices, shards(): lax.all_gather(cross_merge, 'tm', axis=1, tiled=True)  29 us
  transfers between devices with their start and end apart: 10, of which 9 were waited for; matrix products, arithmetic and copies ran while one was open for 4% of the time, Pallas kernels for 0%

commit v1 on v0

--- a/solution.py
+++ b/solution.py
@@ -1,6 +1,10 @@
+import functools
+
 import jax
 import jax.numpy as jnp
 from jax import lax
+from jax.experimental import pallas as pl
+from jax.experimental.pallas import tpu as pltpu
 from jax.sharding import PartitionSpec as P
 
 HEAD_DIM = 64
@@ -142,6 +146,443 @@
     ).astype(jnp.bfloat16)
 
 
+MESH = pl.DeviceIdType.MESH
+UNITS = 8
+KEY, VALUE, QUERY, MERGE, TQUERY, TKEY, TVALUE, TMERGE = range(UNITS)
+PIECES = ((0, 2), (2, 2), (4, 2), (6, 2))
+
+
+def block_kernel(
+    n_tm,
+    n_mp,
+    latents,
+    table,
+    bucket,
+    clearest,
+    visible,
+    shard,
+    out,
+    weights,
+    normed,
+    date_rows,
+    key_value,
+    attended,
+    partial,
+    gathered,
+    middle,
+    second,
+    triple,
+    across,
+    mixed,
+    returned,
+    updated,
+    same_head,
+    own_sem,
+    z_send,
+    z_recv,
+    y_send,
+    y_recv,
+    tm_send,
+    tm_recv,
+    mp_send,
+    mp_recv,
+):
+    f32, bf16 = jnp.float32, jnp.bfloat16
+    g, p, m = lax.axis_index("group"), lax.axis_index("tm"), lax.axis_index("mp")
+    tokens, width = latents.shape
+    depth, local = shard.shape[1], shard.shape[2]
+    half = depth // 2
+    patch, block = tokens // n_tm, tokens // n_mp
+    scale = HEAD_DIM ** (-0.5)
+
+    barrier = pltpu.get_barrier_semaphore()
+    for offset in range(1, n_tm):
+        pl.semaphore_signal(
+            barrier, 1, device_id={"tm": lax.rem(p + offset, n_tm)}, device_id_type=MESH
+        )
+    for offset in range(1, n_mp):
+        pl.semaphore_signal(
+            barrier, 1, device_id={"mp": lax.rem(m + offset, n_mp)}, device_id_type=MESH
+        )
+    pl.semaphore_signal(barrier, 1, device_id={"group": 1 - g}, device_id_type=MESH)
+    pl.semaphore_wait(barrier, n_tm + n_mp - 1)
+
+    own = pltpu.make_async_copy(shard, weights.at[:, p], own_sem)
+    own.start()
+    mine = pl.ds(pl.multiple_of(g * half, 16), half)
+
+    def z_copy(piece, way, step, source, target):
+        first, count = PIECES[piece]
+        units = pl.ds(first, count)
+        slot = weights.at[units, source, mine]
+        return pltpu.make_async_remote_copy(
+            src_ref=shard.at[units, mine] if step == 0 else slot,
+            dst_ref=slot,
+            send_sem=z_send.at[piece, way, step],
+            recv_sem=z_recv.at[piece, way, step],
+            device_id={"tm": target},
+            device_id_type=MESH,
+        )
+
+    def y_copy(piece, way, step, source):
+        first, count = PIECES[piece]
+        slot = weights.at[pl.ds(first, count), source, mine]
+        return pltpu.make_async_remote_copy(
+            src_ref=slot,
+            dst_ref=slot,
+            send_sem=y_send.at[piece, way, step],
+            recv_sem=y_recv.at[piece, way, step],
+            device_id={"group": 1 - g},
+            device_id_type=MESH,
+        )
+
+    def y_arrival(piece, way, step, source):
+        first, count = PIECES[piece]
+        theirs = pl.ds(pl.multiple_of((1 - g) * half, 16), half)
+        slot = weights.at[pl.ds(first, count), source, theirs]
+        return pltpu.make_async_remote_copy(
+            src_ref=slot,
+            dst_ref=slot,
+            send_sem=y_send.at[piece, way, step],
+            recv_sem=y_recv.at[piece, way, step],
+            device_id={"group": 1 - g},
+            device_id_type=MESH,
+        )
+
+    def sends(piece, step, act):
+        @pl.when((p - step >= 0) & (p <= n_tm - 2))
+        def _():
+            act(z_copy(piece, 0, step, p - step, p + 1))
+
+        @pl.when((p + step <= n_tm - 1) & (p >= 1))
+        def _():
+            act(z_copy(piece, 1, step, p + step, p - 1))
+
+    def arrivals(piece, step, act):
+        @pl.when(p - 1 - step >= 0)
+        def _():
+            act(0, p - 1 - step)
+
+        @pl.when(p + 1 + step <= n_tm - 1)
+        def _():
+            act(1, p + 1 + step)
+
+    def send(piece, step):
+        sends(piece, step, lambda copy: copy.start())
+
+    def relay(piece, step):
+        def act(way, source):
+            z_copy(piece, way, step, source, p).wait_recv()
+            y_copy(piece, way, step, source).start()
+
+        arrivals(piece, step, act)
+        if step + 1 < n_tm - 1:
+            send(piece, step + 1)
+
+    def await_piece(piece):
+        for step in range(n_tm - 1):
+            arrivals(
+                piece,
+                step,
+                lambda way, source: y_arrival(piece, way, step, source).wait_recv(),
+            )
+
+    stages = len(PIECES) + n_tm - 1
+
+    def stage(index):
+        for piece in range(len(PIECES)):
+            step = index - piece
+            if 0 <= step < n_tm - 1:
+                relay(piece, step)
+        if index + 2 < len(PIECES):
+            send(index + 2, 0)
+
+    def swap(axis, size, me, sem, source, target):
+        send_sem, recv_sem = (tm_send, tm_recv) if axis == "tm" else (mp_send, mp_recv)
+        copies = []
+        for offset in range(1, size):
+            peer = lax.rem(me + offset, size)
+            copy = pltpu.make_async_remote_copy(
+                src_ref=source(peer),
+                dst_ref=target,
+                send_sem=send_sem.at[sem, offset - 1],
+                recv_sem=recv_sem.at[sem, offset - 1],
+                device_id={axis: peer},
+                device_id_type=MESH,
+            )
+            copy.start()
+            copies.append(copy)
+        return copies
+
+    def finish(copies):
+        for copy in copies:
+            copy.wait()
+
+    def layer_norm(values):
+        centre = jnp.mean(values, axis=-1, keepdims=True)
+        shifted = values - centre
+        variance = jnp.mean(shifted * shifted, axis=-1, keepdims=True)
+        return shifted * lax.rsqrt(variance + 1e-06)
+
+    def project(rows, unit, columns):
+        total = None
+        for source in range(n_tm):
+            term = jnp.dot(
+                rows(source * depth), weights[unit, source], preferred_element_type=f32
+            )
+            total = term if total is None else total + term
+        return total.astype(bf16)
+
+    send(0, 0)
+    send(1, 0)
+    bucket_here = bucket[0]
+    shift_a, scale_a = table[bucket_here, 0:1], table[bucket_here, 1:2]
+
+    step_rows = 32
+
+    def first_norm(index, carry):
+        rows = pl.ds(pl.multiple_of(index * step_rows, step_rows), step_rows)
+        values = latents[rows, :].astype(f32)
+        normed[rows, :] = (layer_norm(values) * (1.0 + scale_a) + shift_a).astype(bf16)
+        return carry
+
+    lax.fori_loop(0, tokens // step_rows, first_norm, 0)
+    date_copies = swap(
+        "tm",
+        n_tm,
+        p,
+        0,
+        lambda peer: normed.at[pl.ds(pl.multiple_of(peer * patch, 16), patch)],
+        date_rows.at[p],
+    )
+    date_rows[p] = normed[pl.ds(pl.multiple_of(p * patch, 16), patch), :]
+    heads_row = lax.broadcasted_iota(jnp.int32, (local, local), 0) >> 6
+    heads_column = lax.broadcasted_iota(jnp.int32, (local, local), 1) >> 6
+    same_head[...] = jnp.where(heads_row == heads_column, 1.0, 0.0).astype(bf16)
+    stage(0)
+    stage(1)
+    stage(2)
+    finish(date_copies)
+    own.wait()
+    await_piece(0)
+    reference_rows = date_rows[clearest[0]]
+    for unit in (KEY, VALUE):
+        key_value[p, unit] = project(
+            lambda start: reference_rows[:, start : start + depth], unit, local
+        )
+    pair_copies = swap("tm", n_tm, p, 1, lambda peer: key_value.at[p], key_value.at[p])
+    stage(3)
+    await_piece(1)
+    queries = project(lambda start: normed[:, start : start + depth], QUERY, local)
+    finish(pair_copies)
+    lane = lax.broadcasted_iota(jnp.int32, (1, 2 * HEAD_DIM), 1)
+    for pair in range(local // (2 * HEAD_DIM)):
+        columns = slice(pair * 2 * HEAD_DIM, (pair + 1) * 2 * HEAD_DIM)
+        pair_query = queries[:, columns]
+        pair_key = key_value[:, KEY, :, columns].reshape(tokens, 2 * HEAD_DIM)
+        pair_value = key_value[:, VALUE, :, columns].reshape(tokens, 2 * HEAD_DIM)
+        halves = []
+        for member in range(2):
+            chosen = (lane >= HEAD_DIM) if member else (lane < HEAD_DIM)
+            picked = jnp.where(chosen, pair_query, jnp.zeros_like(pair_query))
+            scores = (
+                lax.dot_general(
+                    picked, pair_key, (((1,), (1,)), ((), ())), preferred_element_type=f32
+                )
+                * scale
+            )
+            raised = jnp.exp(scores - jnp.max(scores, axis=-1, keepdims=True))
+            probs = (raised / jnp.sum(raised, axis=-1, keepdims=True)).astype(bf16)
+            halves.append(jnp.dot(probs, pair_value, preferred_element_type=f32))
+        attended[:, columns] = jnp.where(lane < HEAD_DIM, halves[0], halves[1]).astype(bf16)
+
+    def merge(rows, unit, which):
+        for source in range(n_tm):
+            term = jnp.dot(rows, weights[unit, source], preferred_element_type=f32)
+            partial[which, :, :, source * depth : (source + 1) * depth] = term.astype(
+                bf16
+            ).reshape(n_mp, block, local)
+        return swap(
+            "mp",
+            n_mp,
+            m,
+            which,
+            lambda peer: partial.at[which, peer],
+            gathered.at[which, m],
+        )
+
+    def merged(which):
+        gathered[which, m] = partial[which, m]
+        total = gathered[which, 0].astype(f32)
+        for source in range(1, n_mp):
+            total = total + gathered[which, source].astype(f32)
+        return total
+
+    cross_copies = merge(attended[...], MERGE, 0)
+    stage(4)
+    finish(cross_copies)
+    block_rows = pl.ds(pl.multiple_of(m * block, 16), block)
+    gate_a = table[bucket_here, 2:3]
+    shift_b, scale_b = table[bucket_here, 3:4], table[bucket_here, 4:5]
+    middle[...] = latents[block_rows, :].astype(f32) + gate_a * merged(0)
+    second[m] = (layer_norm(middle[...]) * (1.0 + scale_b) + shift_b).astype(bf16)
+    second_copies = swap("mp", n_mp, m, 2, lambda peer: second.at[m], second.at[m])
+    stage(5)
+    finish(second_copies)
+    triple_copies = []
+    for index, unit in enumerate((TQUERY, TKEY, TVALUE)):
+        if index == 0:
+            await_piece(2)
+        if index == 2:
+            await_piece(3)
+        triple[index] = project(
+            lambda start: second[:, :, start : start + depth].reshape(tokens, depth), unit, local
+        ).reshape(n_tm, patch, local)
+        across[p, index] = triple[index, p]
+        triple_copies += swap(
+            "tm",
+            n_tm,
+            p,
+            2 + index,
+            lambda peer: triple.at[index, peer],
+            across.at[p, index],
+        )
+    finish(triple_copies)
+    seen = visible[pl.ds(pl.multiple_of(p * patch, 16), patch), :]
+    time_key = across[:, 1].astype(f32)
+    for date in range(n_tm):
+        products = (across[date, 0].astype(f32)[None] * time_key).reshape(n_tm * patch, local)
+        upper = products.astype(bf16)
+        lower = (products - upper.astype(f32)).astype(bf16)
+        scores = (
+            jnp.dot(upper, same_head[...], preferred_element_type=f32)
+            + jnp.dot(lower, same_head[...], preferred_element_type=f32)
+        ) * scale
+        scores = scores.reshape(n_tm, patch, local)
+        shown = [
+            jnp.where(seen[:, other : other + 1] > 0.5, scores[other], -1e30)
+            for other in range(n_tm)
+        ]
+        highest = functools.reduce(jnp.maximum, shown)
+        raised = [jnp.exp(score - highest) for score in shown]
+        total = functools.reduce(jnp.add, raised)
+        result = None
+        for other in range(n_tm):
+            prob = (raised[other] / total).astype(bf16).astype(f32)
+            term = prob * across[other, 2].astype(f32)
+            result = term if result is None else result + term
+        mixed[date] = result.astype(bf16)
+    mixed_copies = swap("tm", n_tm, p, 5, lambda peer: mixed.at[peer], returned.at[p])
+    returned[p] = mixed[p]
+    finish(mixed_copies)
+    time_copies = merge(returned[...].reshape(tokens, local), TMERGE, 1)
+    finish(time_copies)
+    gate_b = table[bucket_here, 5:6]
+    updated[m] = (middle[...] + gate_b * merged(1)).astype(bf16)
+    last_copies = swap("mp", n_mp, m, 3, lambda peer: updated.at[m], updated.at[m])
+    finish(last_copies)
+    out[...] = updated[...].reshape(tokens, width)
+
+    for piece in range(len(PIECES)):
+        for step in range(n_tm - 1):
+            sends(piece, step, lambda copy: copy.wait_send())
+            arrivals(
+                piece,
+                step,
+                lambda way, source: y_copy(piece, way, step, source).wait_send(),
+            )
+
+
+def fused(
+    n_tm,
+    n_mp,
+    latents,
+    gsd_table,
+    gsd_bucket,
+    clearest,
+    clouds,
+    cross_query,
+    cross_pairs,
+    cross_merge,
+    time_triple,
+    time_merge,
+):
+    tokens, width = latents.shape[2:]
+    depth, local = cross_query.shape
+    shard = jnp.stack(
+        [
+            cross_pairs[:, 0],
+            cross_pairs[:, 1],
+            cross_query,
+            cross_merge,
+            time_triple[:, 0],
+            time_triple[:, 1],
+            time_triple[:, 2],
+            time_merge,
+        ]
+    )
+    visible = (clouds[0] == 0).astype(jnp.float32).T
+    patch, block = tokens // n_tm, tokens // n_mp
+    bf16, f32 = jnp.bfloat16, jnp.float32
+    vmem = pl.BlockSpec(memory_space=pltpu.VMEM)
+    smem = pl.BlockSpec(memory_space=pltpu.SMEM)
+    dma = pltpu.SemaphoreType.DMA
+    pieces = len(PIECES)
+    result = pl.pallas_call(
+        functools.partial(block_kernel, n_tm, n_mp),
+        out_shape=jax.ShapeDtypeStruct((tokens, width), bf16),
+        in_specs=[vmem, vmem, smem, smem, vmem, pl.BlockSpec(memory_space=pl.ANY)],
+        out_specs=vmem,
+        scratch_shapes=[
+            pltpu.VMEM((UNITS, n_tm, depth, local), bf16),
+            pltpu.VMEM((tokens, width), bf16),
+            pltpu.VMEM((n_tm, patch, width), bf16),
+            pltpu.VMEM((n_tm, 2, patch, local), bf16),
+            pltpu.VMEM((tokens, local), bf16),
+            pltpu.VMEM((2, n_mp, block, width), bf16),
+            pltpu.VMEM((2, n_mp, block, width), bf16),
+            pltpu.VMEM((block, width), f32),
+            pltpu.VMEM((n_mp, block, width), bf16),
+            pltpu.VMEM((3, n_tm, patch, local), bf16),
+            pltpu.VMEM((n_tm, 3, patch, local), bf16),
+            pltpu.VMEM((n_tm, patch, local), bf16),
+            pltpu.VMEM((n_tm, patch, local), bf16),
+            pltpu.VMEM((n_mp, block, width), bf16),
+            pltpu.VMEM((local, local), bf16),
+            dma,
+            dma((pieces, 2, n_tm - 1)),
+            dma((pieces, 2, n_tm - 1)),
+            dma((pieces, 2, n_tm - 1)),
+            dma((pieces, 2, n_tm - 1)),
+            dma((6, n_tm - 1)),
+            dma((6, n_tm - 1)),
+            dma((4, n_mp - 1)),
+            dma((4, n_mp - 1)),
+        ],
+        compiler_params=pltpu.CompilerParams(
+            collective_id=0, has_side_effects=True, vmem_limit_bytes=56 * 1024 * 1024
+        ),
+    )(latents[0, 0], gsd_table, gsd_bucket.reshape(1), clearest, visible, shard)
+    return result[None, None]
+
+
+def fits(mesh, latents, cross_query):
+    n_tm, n_mp = mesh.shape["tm"], mesh.shape["mp"]
+    tokens, width = latents.shape[2:]
+    depth, local = width // n_tm, width // n_mp
+    return (
+        mesh.shape["group"] == 2
+        and latents.shape[0] == 2
+        and latents.shape[1] == n_tm
+        and n_tm <= 8
+        and n_mp >= 2
+        and tokens % (16 * n_tm) == 0
+        and tokens % (16 * n_mp) == 0
+        and depth % 128 == 0
+        and depth == local
+    )
+
+
 def solution(mesh):
     placed = (
         P("group", "tm", None, None),
@@ -155,6 +596,17 @@
         P("tm", None, "mp"),
         P("mp", "tm"),
     )
-    return jax.shard_map(
-        shards, mesh=mesh, in_specs=placed, out_specs=P("group", "tm", None, None), check_vma=False
-    )
+
+    def run(*args):
+        body = shards
+        if fits(mesh, args[0], args[5]):
+            body = functools.partial(fused, mesh.shape["tm"], mesh.shape["mp"])
+        return jax.shard_map(
+            body,
+            mesh=mesh,
+            in_specs=placed,
+            out_specs=P("group", "tm", None, None),
+            check_vma=False,
+        )(*args)
+
+    return run

time: 376 us -> 154 us (0.41)
  waiting for transfers between devices: 322 us -> 0 us
  Pallas kernels: 0 us -> 143 us
  between operations: 15 us -> 1.43 us
  matrix products: 12.9 us -> 0 us
  starting transfers between devices: 7.84 us -> 0 us
  other arithmetic: 6.42 us -> 0.67 us
  local copies, waits for them, and re-layouts: 10.5 us -> 6.68 us
    all_gather x5 -> x0, waiting for transfers between devices: 178 us -> none  [the longest x1 69.5 us: shards(): lax.all_gather(time_triple, 'tm', axis=0, tiled=True)]
    pallas_call x0 -> x1, Pallas kernels: none -> 143 us  [fused(): pl.pallas_call(functools.partial(block_kernel, n_tm, n_mp), out_shape=jax...]
    psum x3 -> x0, waiting for transfers between devices: 105 us -> none  [the longest x1 36.6 us: broadcast(): return lax.psum(block, axis)]
    all_to_all x2 -> x0, waiting for transfers between devices: 37.3 us -> none  [the longest x1 31.1 us: shards(): lax.all_to_all(triple, 'tm', split_axis=2, concat_axis=1, tiled=True)]
    dot_general x8 -> x0, matrix products: 12.2 us -> none  [the longest x1 3.25 us: shards(): jnp.einsum('nd,dce->nce', normed_two.reshape(stacks * seq_tokens, model_w...]
    all_to_all x2 -> x0, starting transfers between devices: 7.56 us -> none  [the longest x1 4.19 us: shards(): lax.all_to_all(triple, 'tm', split_axis=2, concat_axis=1, tiled=True)]
    reshape x3 -> x0, local copies, waits for them, and re-layouts: 5.09 us -> none  [the longest x1 2.7 us: shards(): patches.reshape(stacks, date_count, patch_count, 3, local_heads, HEAD_DIM)]
  transfers between devices with their start and end apart: 10 -> 0, of which waited for: 9 -> 0; matrix products, arithmetic and copies ran while one was open for 4% -> 0% of each run, Pallas kernels for 0% -> 0%
where the time goes in v1:
time: 154 us; the launch traced here: 152 us
  Pallas kernels  143 us (93%)
  local copies, waits for them, and re-layouts  6.68 us (4%)
    pallas_call x1, Pallas kernels, fused(): pl.pallas_call(functools.partial(block_kernel, n_tm, n_mp), out_shape=jax...  143 us
    unnamed x23, local copies, waits for them, and re-layouts  4.09 us

profile of v1, /device:TPU:0, one launch (start us, length us, event | category | flops | bytes accessed | tf_op | source)
XLA Modules:
  0.0 151.8 jit_solution(5828694918761347467)
XLA Ops:
  0.0 0.0 copy-start.2
  0.0 0.0 copy-start.3
  0.0 0.0 copy-start.1
  0.0 2.4 %fusion.2 = (bf16[384,1,384]{2,1,0:T(2,128)(2,1)S(1)}, bf16[384,1,384]{2,1,0:T(2,128)(2,1)S(1)}) fusion(bf16[384,2,384]{2,1,0:T(2,128)(2,1)} %param.16), kind=kLoop, calls=%fused_computation.12 | loop fusion | bytes 1179648 | tf_op jit(solution)/shard_map/slice | solution.py:515
  2.4 0.0 copy-start.4
  2.4 0.0 copy-start.5
  2.5 0.0 copy-start.6
  2.5 0.1 fusion
  2.5 0.0 copy-done.2
  2.6 0.0 copy-done.3
  2.7 0.0 copy-done.1
  2.8 0.5 copy-done.4
  3.4 0.1 copy-done.5
  3.4 0.0 copy-start
  3.4 1.1 copy.19.table
  4.6 0.0 copy-done.6
  4.6 0.2 copy.16
  4.7 0.7 convert_bitcast_fusion.visible
  6.7 0.0 copy-done
  6.7 143.0 %shard_map.100 = bf16[256,1536]{1,0:T(8,128)(2,1)} custom-call(bf16[256,1536]{1,0:T(8,128)(2,1)} %bitcast.29, f32[8,6,1536]{2,1,0:T(8,128)} %copy.19.table, s32[1]{0:T(128)} %bitcast.27.bucket, s32[1]{0:T(128)S(6)} %copy.37.clearest, f32[256,4]{1,0:T(8,128)} %convert_bitcast_fusion.visible, bf16[8,384,384]{2,1,0:T(8,128)(2,1)} %copy-done), custom_call_target="tpu_custom_call" | custom-call | tf_op jit(solution)/shard_map/pallas_call | solution.py:531
  149.7 2.1 %copy.38 = bf16[1,1,256,1536]{3,2,1,0:T(8,128)(2,1)} copy(bf16[1,1,256,1536]{3,2,1,0:T(8,128)(2,1)} %bitcast.28) | data formatting | bytes 1572864
  (8 shorter events, 0.3 us)
Async XLA Ops:
  0.0 2.5 %copy-start.2 = (bf16[384,384]{1,0:T(8,128)(2,1)S(1)}, bf16[384,384]{1,0:T(8,128)(2,1)}, u32[]{:S(2)}) copy-start(bf16[384,384]{1,0:T(8,128)(2,1)} %param.15) | copy-start | bytes 884740
  0.0 2.6 %copy-start.3 = (bf16[384,384]{1,0:T(8,128)(2,1)S(1)}, bf16[384,384]{1,0:T(8,128)(2,1)}, u32[]{:S(2)}) copy-start(bf16[384,384]{1,0:T(8,128)(2,1)} %param.17) | copy-start | bytes 884740
  0.0 2.7 %copy-start.1 = (bf16[384,3,384]{2,0,1:T(8,128)(2,1)S(1)}, bf16[384,3,384]{2,0,1:T(8,128)(2,1)}, u32[]{:S(2)}) copy-start(bf16[384,3,384]{2,0,1:T(8,128)(2,1)} %param.18) | copy-start | bytes 2654212
  2.4 1.0 copy-start.4
  2.4 1.0 copy-start.5
  2.5 2.1 %copy-start.6 = (s32[1,4,256]{2,1,0:T(4,128)S(1)}, s32[1,4,256]{2,1,0:T(4,128)}, u32[]{:S(2)}) copy-start(s32[1,4,256]{2,1,0:T(4,128)} %param.14) | copy-start | bytes 12292
  3.4 3.3 %copy-start = (bf16[8,384,384]{2,1,0:T(8,128)(2,1)}, bf16[8,384,384]{2,1,0:T(8,128)(2,1)S(1)}, u32[]{:S(2)}) copy-start(bf16[8,384,384]{2,1,0:T(8,128)(2,1)S(1)} %bitcast_dynamic-update-slice_fusion.shard) | copy-start | bytes 7077892

commit v2 on v1

--- a/solution.py
+++ b/solution.py
@@ -147,9 +147,11 @@
 
 
 MESH = pl.DeviceIdType.MESH
-UNITS = 8
-KEY, VALUE, QUERY, MERGE, TQUERY, TKEY, TVALUE, TMERGE = range(UNITS)
-PIECES = ((0, 2), (2, 2), (4, 2), (6, 2))
+UNITS = 6
+QUERY, MERGE, TQUERY, TKEY, TVALUE, TMERGE = range(UNITS)
+KEY, VALUE = 0, 1
+PIECES = ((QUERY, 1), (MERGE, 1), (TQUERY, 1), (TKEY, 1), (TVALUE, 1), (TMERGE, 1))
+PARTS = 2
 
 
 def block_kernel(
@@ -161,10 +163,15 @@
     clearest,
     visible,
     shard,
+    pair_shard,
     out,
     weights,
+    pair_weights,
     normed,
     date_rows,
+    reference_rows,
+    pair_partial,
+    pair_terms,
     key_value,
     attended,
     partial,
@@ -178,6 +185,7 @@
     updated,
     same_head,
     own_sem,
+    pair_sem,
     z_send,
     z_recv,
     y_send,
@@ -186,6 +194,8 @@
     tm_recv,
     mp_send,
     mp_recv,
+    share_send,
+    share_recv,
 ):
     f32, bf16 = jnp.float32, jnp.bfloat16
     g, p, m = lax.axis_index("group"), lax.axis_index("tm"), lax.axis_index("mp")
@@ -209,6 +219,8 @@
 
     own = pltpu.make_async_copy(shard, weights.at[:, p], own_sem)
     own.start()
+    own_pair = pltpu.make_async_copy(pair_shard, pair_weights, pair_sem)
+    own_pair.start()
     mine = pl.ds(pl.multiple_of(g * half, 16), half)
 
     def z_copy(piece, way, step, source, target):
@@ -314,6 +326,39 @@
             copies.append(copy)
         return copies
 
+    mate = m + 1 - 2 * lax.rem(m, 2)
+    across_x = lax.rem(m + 2, n_mp)
+
+    def share_copy(buffer, which, part, hop, slot, target):
+        rows = block // PARTS
+        place = buffer.at[slot, pl.ds(part * rows, rows)]
+        return pltpu.make_async_remote_copy(
+            src_ref=place,
+            dst_ref=place,
+            send_sem=share_send.at[which, part, hop],
+            recv_sem=share_recv.at[which, part, hop],
+            device_id={"mp": target},
+            device_id_type=MESH,
+        )
+
+    def share_start(buffer, which):
+        for part in range(PARTS):
+            share_copy(buffer, which, part, 0, m, across_x).start()
+        for part in range(PARTS):
+            share_copy(buffer, which, part, 1, m, mate).start()
+
+    def share_finish(buffer, which):
+        for part in range(PARTS):
+            share_copy(buffer, which, part, 0, across_x, m).wait_recv()
+            share_copy(buffer, which, part, 2, across_x, mate).start()
+        for part in range(PARTS):
+            share_copy(buffer, which, part, 1, mate, m).wait_recv()
+            share_copy(buffer, which, part, 2, lax.rem(mate + 2, n_mp), m).wait_recv()
+        for part in range(PARTS):
+            share_copy(buffer, which, part, 0, m, across_x).wait_send()
+            share_copy(buffer, which, part, 1, m, mate).wait_send()
+            share_copy(buffer, which, part, 2, across_x, mate).wait_send()
+
     def finish(copies):
         for copy in copies:
             copy.wait()
@@ -347,33 +392,48 @@
         return carry
 
     lax.fori_loop(0, tokens // step_rows, first_norm, 0)
+    block_rows = pl.ds(pl.multiple_of(m * block, 16), block)
     date_copies = swap(
         "tm",
         n_tm,
         p,
         0,
-        lambda peer: normed.at[pl.ds(pl.multiple_of(peer * patch, 16), patch)],
+        lambda peer: normed.at[block_rows, pl.ds(pl.multiple_of(peer * depth, 128), depth)],
         date_rows.at[p],
     )
-    date_rows[p] = normed[pl.ds(pl.multiple_of(p * patch, 16), patch), :]
+    date_rows[p] = normed[block_rows, pl.ds(pl.multiple_of(p * depth, 128), depth)]
     heads_row = lax.broadcasted_iota(jnp.int32, (local, local), 0) >> 6
     heads_column = lax.broadcasted_iota(jnp.int32, (local, local), 1) >> 6
     same_head[...] = jnp.where(heads_row == heads_column, 1.0, 0.0).astype(bf16)
     stage(0)
+    finish(date_copies)
+    reference_rows[m] = date_rows[clearest[0]]
+    row_copies = swap(
+        "mp", n_mp, m, 2, lambda peer: reference_rows.at[m], reference_rows.at[m]
+    )
     stage(1)
+    finish(row_copies)
+    own_pair.wait()
+    for unit in (KEY, VALUE):
+        term = jnp.dot(
+            reference_rows[...].reshape(tokens, depth),
+            pair_weights[unit],
+            preferred_element_type=f32,
+        )
+        pair_partial[:, unit] = term.astype(bf16).reshape(n_tm, patch, local)
+    term_copies = swap("tm", n_tm, p, 1, lambda peer: pair_partial.at[peer], pair_terms.at[p])
+    pair_terms[p] = pair_partial[p]
     stage(2)
-    finish(date_copies)
+    finish(term_copies)
+    pair_total = pair_terms[0].astype(f32)
+    for source in range(1, n_tm):
+        pair_total = pair_total + pair_terms[source].astype(f32)
+    key_value[p] = pair_total.astype(bf16)
+    pair_copies = swap("tm", n_tm, p, 2, lambda peer: key_value.at[p], key_value.at[p])
     own.wait()
     await_piece(0)
-    reference_rows = date_rows[clearest[0]]
-    for unit in (KEY, VALUE):
-        key_value[p, unit] = project(
-            lambda start: reference_rows[:, start : start + depth], unit, local
-        )
-    pair_copies = swap("tm", n_tm, p, 1, lambda peer: key_value.at[p], key_value.at[p])
+    queries = project(lambda start: normed[:, start : start + depth], QUERY, local)
     stage(3)
-    await_piece(1)
-    queries = project(lambda start: normed[:, start : start + depth], QUERY, local)
     finish(pair_copies)
     lane = lax.broadcasted_iota(jnp.int32, (1, 2 * HEAD_DIM), 1)
     for pair in range(local // (2 * HEAD_DIM)):
@@ -418,23 +478,20 @@
             total = total + gathered[which, source].astype(f32)
         return total
 
+    await_piece(1)
     cross_copies = merge(attended[...], MERGE, 0)
     stage(4)
     finish(cross_copies)
-    block_rows = pl.ds(pl.multiple_of(m * block, 16), block)
     gate_a = table[bucket_here, 2:3]
     shift_b, scale_b = table[bucket_here, 3:4], table[bucket_here, 4:5]
     middle[...] = latents[block_rows, :].astype(f32) + gate_a * merged(0)
     second[m] = (layer_norm(middle[...]) * (1.0 + scale_b) + shift_b).astype(bf16)
-    second_copies = swap("mp", n_mp, m, 2, lambda peer: second.at[m], second.at[m])
+    share_start(second, 0)
     stage(5)
-    finish(second_copies)
+    share_finish(second, 0)
     triple_copies = []
     for index, unit in enumerate((TQUERY, TKEY, TVALUE)):
-        if index == 0:
-            await_piece(2)
-        if index == 2:
-            await_piece(3)
+        await_piece(unit)
         triple[index] = project(
             lambda start: second[:, :, start : start + depth].reshape(tokens, depth), unit, local
         ).reshape(n_tm, patch, local)
@@ -443,10 +500,12 @@
             "tm",
             n_tm,
             p,
-            2 + index,
+            3 + index,
             lambda peer: triple.at[index, peer],
             across.at[p, index],
         )
+        if index < 2:
+            stage(6 + index)
     finish(triple_copies)
     seen = visible[pl.ds(pl.multiple_of(p * patch, 16), patch), :]
     time_key = across[:, 1].astype(f32)
@@ -472,15 +531,16 @@
             term = prob * across[other, 2].astype(f32)
             result = term if result is None else result + term
         mixed[date] = result.astype(bf16)
-    mixed_copies = swap("tm", n_tm, p, 5, lambda peer: mixed.at[peer], returned.at[p])
+    mixed_copies = swap("tm", n_tm, p, 6, lambda peer: mixed.at[peer], returned.at[p])
     returned[p] = mixed[p]
     finish(mixed_copies)
+    await_piece(5)
     time_copies = merge(returned[...].reshape(tokens, local), TMERGE, 1)
     finish(time_copies)
     gate_b = table[bucket_here, 5:6]
     updated[m] = (middle[...] + gate_b * merged(1)).astype(bf16)
-    last_copies = swap("mp", n_mp, m, 3, lambda peer: updated.at[m], updated.at[m])
-    finish(last_copies)
+    share_start(updated, 1)
+    share_finish(updated, 1)
     out[...] = updated[...].reshape(tokens, width)
 
     for piece in range(len(PIECES)):
@@ -511,8 +571,6 @@
     depth, local = cross_query.shape
     shard = jnp.stack(
         [
-            cross_pairs[:, 0],
-            cross_pairs[:, 1],
             cross_query,
             cross_merge,
             time_triple[:, 0],
@@ -521,6 +579,7 @@
             time_merge,
         ]
     )
+    pair_shard = jnp.stack([cross_pairs[:, 0], cross_pairs[:, 1]])
     visible = (clouds[0] == 0).astype(jnp.float32).T
     patch, block = tokens // n_tm, tokens // n_mp
     bf16, f32 = jnp.bfloat16, jnp.float32
@@ -531,12 +590,16 @@
     result = pl.pallas_call(
         functools.partial(block_kernel, n_tm, n_mp),
         out_shape=jax.ShapeDtypeStruct((tokens, width), bf16),
-        in_specs=[vmem, vmem, smem, smem, vmem, pl.BlockSpec(memory_space=pl.ANY)],
+        in_specs=[vmem, vmem, smem, smem, vmem] + [pl.BlockSpec(memory_space=pl.ANY)] * 2,
         out_specs=vmem,
         scratch_shapes=[
             pltpu.VMEM((UNITS, n_tm, depth, local), bf16),
+            pltpu.VMEM((2, depth, local), bf16),
             pltpu.VMEM((tokens, width), bf16),
-            pltpu.VMEM((n_tm, patch, width), bf16),
+            pltpu.VMEM((n_tm, block, depth), bf16),
+            pltpu.VMEM((n_mp, block, depth), bf16),
+            pltpu.VMEM((n_tm, 2, patch, local), bf16),
+            pltpu.VMEM((n_tm, 2, patch, local), bf16),
             pltpu.VMEM((n_tm, 2, patch, local), bf16),
             pltpu.VMEM((tokens, local), bf16),
             pltpu.VMEM((2, n_mp, block, width), bf16),
@@ -550,19 +613,22 @@
             pltpu.VMEM((n_mp, block, width), bf16),
             pltpu.VMEM((local, local), bf16),
             dma,
+            dma,
             dma((pieces, 2, n_tm - 1)),
             dma((pieces, 2, n_tm - 1)),
             dma((pieces, 2, n_tm - 1)),
             dma((pieces, 2, n_tm - 1)),
-            dma((6, n_tm - 1)),
-            dma((6, n_tm - 1)),
-            dma((4, n_mp - 1)),
-            dma((4, n_mp - 1)),
+            dma((7, n_tm - 1)),
+            dma((7, n_tm - 1)),
+            dma((3, n_mp - 1)),
+            dma((3, n_mp - 1)),
+            dma((2, PARTS, 3)),
+            dma((2, PARTS, 3)),
         ],
         compiler_params=pltpu.CompilerParams(
             collective_id=0, has_side_effects=True, vmem_limit_bytes=56 * 1024 * 1024
         ),
-    )(latents[0, 0], gsd_table, gsd_bucket.reshape(1), clearest, visible, shard)
+    )(latents[0, 0], gsd_table, gsd_bucket.reshape(1), clearest, visible, shard, pair_shard)
     return result[None, None]
 
 
@@ -575,9 +641,9 @@
         and latents.shape[0] == 2
         and latents.shape[1] == n_tm
         and n_tm <= 8
-        and n_mp >= 2
+        and n_mp == 4
         and tokens % (16 * n_tm) == 0
-        and tokens % (16 * n_mp) == 0
+        and tokens % (16 * PARTS * n_mp) == 0
         and depth % 128 == 0
         and depth == local
     )

time: 154 us -> 129 us (0.84); the launches traced: 152 us -> 129 us
  Pallas kernels: 143 us -> 117 us
  other arithmetic: 0.67 us -> 2.25 us
    pallas_call x1, Pallas kernels: 143 us -> 117 us  [fused(): pl.pallas_call(functools.partial(block_kernel, n_tm, n_mp), out_shape=jax...]
    unnamed x23 -> x15, local copies, waits for them, and re-layouts: 4.09 us -> 6.58 us
    slice x1, local copies, waits for them, and re-layouts: 2.37 us -> 0.82 us  [fused(): pair_shard = jnp.stack([cross_pairs[:, 0], cross_pairs[:, 1]])]
where the time goes in v2:
time: 129 us
  Pallas kernels  117 us (91%)
  local copies, waits for them, and re-layouts  7.72 us (6%)
  other arithmetic  2.25 us (2%)
  between operations  1.4 us (1%)
    pallas_call x1, Pallas kernels, fused(): pl.pallas_call(functools.partial(block_kernel, n_tm, n_mp), out_shape=jax...  117 us
    unnamed x15, local copies, waits for them, and re-layouts  6.58 us

profile of v2, /device:TPU:0, one launch (start us, length us, event | category | flops | bytes accessed | tf_op | source)
XLA Modules:
  0.0 128.6 jit_solution(15027634123211283621)
XLA Ops:
  0.0 0.0 copy-start.2
  0.0 0.0 copy-start.3
  0.0 2.0 %copy.19.table = f32[8,6,1536]{2,1,0:T(8,128)} copy(f32[8,6,1536]{2,0,1:T(8,128)} %param.11) | data formatting | bytes 589824 | tf_op args[1]
  3.3 0.7 broadcast_compare_fusion
  4.0 0.2 copy.16
  4.2 0.7 convert_bitcast_fusion.visible
  4.8 0.0 copy-start.1
  4.8 1.1 bitcast_dynamic-update-slice_fusion.5
  5.9 1.0 bitcast_dynamic-update-slice_fusion.4
  6.9 0.0 copy-done.2
  7.1 0.0 copy-done.3
  7.2 0.0 copy-done.1
  7.2 0.0 copy-start
  7.2 0.8 fusion
  8.0 0.1 copy_bitcast_fusion
  8.1 0.3 copy-done
  8.4 0.9 pad_maximum_fusion.pair_shard
  9.3 117.3 %shard_map.100 = bf16[256,1536]{1,0:T(8,128)(2,1)} custom-call(bf16[256,1536]{1,0:T(8,128)(2,1)} %bitcast.25, f32[8,6,1536]{2,1,0:T(8,128)} %copy.19.table, s32[1]{0:T(128)} %bitcast.23.bucket, s32[1]{0:T(128)S(6)} %copy.31.clearest, f32[256,4]{1,0:T(8,128)} %convert_bitcast_fusion.visible, bf16[6,384,384]{2,1,0:T(8,128)(2,1)} %copy-done, ...), custom_call_target="tpu_custom_call" | custom-call | tf_op jit(solution)/shard_map/pallas_call | solution.py:590
  126.6 2.1 %copy.32 = bf16[1,1,256,1536]{3,2,1,0:T(8,128)(2,1)} copy(bf16[1,1,256,1536]{3,2,1,0:T(8,128)(2,1)} %bitcast.24) | data formatting | bytes 1572864
  (4 shorter events, 0.2 us)
Async XLA Ops:
  0.0 6.9 %copy-start.2 = (bf16[384,3,384]{2,0,1:T(8,128)(2,1)S(1)}, bf16[384,3,384]{2,0,1:T(8,128)(2,1)}, u32[]{:S(2)}) copy-start(bf16[384,3,384]{2,0,1:T(8,128)(2,1)} %param.18) | copy-start | bytes 2654212
  0.0 7.1 %copy-start.3 = (bf16[384,384]{1,0:T(8,128)(2,1)S(1)}, bf16[384,384]{1,0:T(8,128)(2,1)}, u32[]{:S(2)}) copy-start(bf16[384,384]{1,0:T(8,128)(2,1)} %param.19) | copy-start | bytes 884740
  4.8 2.3 %copy-start.1 = (bf16[384,2,384]{2,1,0:T(2,128)(2,1)S(1)}, bf16[384,2,384]{2,1,0:T(2,128)(2,1)}, u32[]{:S(2)}) copy-start(bf16[384,2,384]{2,1,0:T(2,128)(2,1)} %param.16) | copy-start | bytes 1769476
  7.2 1.2 copy-start

commit v3 on v2

--- a/solution.py
+++ b/solution.py
@@ -150,7 +150,7 @@
 UNITS = 6
 QUERY, MERGE, TQUERY, TKEY, TVALUE, TMERGE = range(UNITS)
 KEY, VALUE = 0, 1
-PIECES = ((QUERY, 1), (MERGE, 1), (TQUERY, 1), (TKEY, 1), (TVALUE, 1), (TMERGE, 1))
+PIECES = (QUERY, MERGE, TQUERY, TKEY, TVALUE, TMERGE)
 PARTS = 2
 
 
@@ -161,8 +161,11 @@
     table,
     bucket,
     clearest,
-    visible,
-    shard,
+    clouds,
+    query_shard,
+    merge_shard,
+    triple_shard,
+    time_shard,
     pair_shard,
     out,
     weights,
@@ -200,7 +203,7 @@
     f32, bf16 = jnp.float32, jnp.bfloat16
     g, p, m = lax.axis_index("group"), lax.axis_index("tm"), lax.axis_index("mp")
     tokens, width = latents.shape
-    depth, local = shard.shape[1], shard.shape[2]
+    depth, local = query_shard.shape[0], query_shard.shape[1]
     half = depth // 2
     patch, block = tokens // n_tm, tokens // n_mp
     scale = HEAD_DIM ** (-0.5)
@@ -217,18 +220,27 @@
     pl.semaphore_signal(barrier, 1, device_id={"group": 1 - g}, device_id_type=MESH)
     pl.semaphore_wait(barrier, n_tm + n_mp - 1)
 
-    own = pltpu.make_async_copy(shard, weights.at[:, p], own_sem)
-    own.start()
+    own_copies = [
+        pltpu.make_async_copy(query_shard, weights.at[QUERY, p], own_sem.at[0]),
+        pltpu.make_async_copy(merge_shard, weights.at[MERGE, p], own_sem.at[1]),
+        pltpu.make_async_copy(triple_shard, weights.at[pl.ds(TQUERY, 3), p], own_sem.at[2]),
+        pltpu.make_async_copy(time_shard, weights.at[TMERGE, p], own_sem.at[3]),
+    ]
+    origins = (
+        query_shard,
+        merge_shard,
+        triple_shard.at[0],
+        triple_shard.at[1],
+        triple_shard.at[2],
+        time_shard,
+    )
     own_pair = pltpu.make_async_copy(pair_shard, pair_weights, pair_sem)
-    own_pair.start()
     mine = pl.ds(pl.multiple_of(g * half, 16), half)
 
     def z_copy(piece, way, step, source, target):
-        first, count = PIECES[piece]
-        units = pl.ds(first, count)
-        slot = weights.at[units, source, mine]
+        slot = weights.at[PIECES[piece], source, mine]
         return pltpu.make_async_remote_copy(
-            src_ref=shard.at[units, mine] if step == 0 else slot,
+            src_ref=origins[piece].at[mine] if step == 0 else slot,
             dst_ref=slot,
             send_sem=z_send.at[piece, way, step],
             recv_sem=z_recv.at[piece, way, step],
@@ -237,8 +249,7 @@
         )
 
     def y_copy(piece, way, step, source):
-        first, count = PIECES[piece]
-        slot = weights.at[pl.ds(first, count), source, mine]
+        slot = weights.at[PIECES[piece], source, mine]
         return pltpu.make_async_remote_copy(
             src_ref=slot,
             dst_ref=slot,
@@ -249,9 +260,8 @@
         )
 
     def y_arrival(piece, way, step, source):
-        first, count = PIECES[piece]
         theirs = pl.ds(pl.multiple_of((1 - g) * half, 16), half)
-        slot = weights.at[pl.ds(first, count), source, theirs]
+        slot = weights.at[PIECES[piece], source, theirs]
         return pltpu.make_async_remote_copy(
             src_ref=slot,
             dst_ref=slot,
@@ -379,19 +389,23 @@
         return total.astype(bf16)
 
     send(0, 0)
-    send(1, 0)
-    bucket_here = bucket[0]
-    shift_a, scale_a = table[bucket_here, 0:1], table[bucket_here, 1:2]
+    for copy in own_copies:
+        copy.start()
+    own_pair.start()
+    bucket_here = pl.ds(bucket[0], 1)
+    shift_a, scale_a = table[0, bucket_here, :], table[1, bucket_here, :]
 
     step_rows = 32
+    steps, own_steps = tokens // step_rows, block // step_rows
 
     def first_norm(index, carry):
-        rows = pl.ds(pl.multiple_of(index * step_rows, step_rows), step_rows)
+        start = lax.rem(index + m * own_steps, steps) * step_rows
+        rows = pl.ds(pl.multiple_of(start, step_rows), step_rows)
         values = latents[rows, :].astype(f32)
         normed[rows, :] = (layer_norm(values) * (1.0 + scale_a) + shift_a).astype(bf16)
         return carry
 
-    lax.fori_loop(0, tokens // step_rows, first_norm, 0)
+    lax.fori_loop(0, own_steps, first_norm, 0)
     block_rows = pl.ds(pl.multiple_of(m * block, 16), block)
     date_copies = swap(
         "tm",
@@ -402,16 +416,17 @@
         date_rows.at[p],
     )
     date_rows[p] = normed[block_rows, pl.ds(pl.multiple_of(p * depth, 128), depth)]
+    send(1, 0)
+    lax.fori_loop(own_steps, steps, first_norm, 0)
     heads_row = lax.broadcasted_iota(jnp.int32, (local, local), 0) >> 6
     heads_column = lax.broadcasted_iota(jnp.int32, (local, local), 1) >> 6
     same_head[...] = jnp.where(heads_row == heads_column, 1.0, 0.0).astype(bf16)
-    stage(0)
     finish(date_copies)
     reference_rows[m] = date_rows[clearest[0]]
     row_copies = swap(
-        "mp", n_mp, m, 2, lambda peer: reference_rows.at[m], reference_rows.at[m]
-    )
-    stage(1)
+        "mp", n_mp, m, 4, lambda peer: reference_rows.at[m], reference_rows.at[m]
+    )
+    stage(0)
     finish(row_copies)
     own_pair.wait()
     for unit in (KEY, VALUE):
@@ -423,14 +438,16 @@
         pair_partial[:, unit] = term.astype(bf16).reshape(n_tm, patch, local)
     term_copies = swap("tm", n_tm, p, 1, lambda peer: pair_partial.at[peer], pair_terms.at[p])
     pair_terms[p] = pair_partial[p]
-    stage(2)
+    stage(1)
     finish(term_copies)
     pair_total = pair_terms[0].astype(f32)
     for source in range(1, n_tm):
         pair_total = pair_total + pair_terms[source].astype(f32)
     key_value[p] = pair_total.astype(bf16)
     pair_copies = swap("tm", n_tm, p, 2, lambda peer: key_value.at[p], key_value.at[p])
-    own.wait()
+    stage(2)
+    for copy in own_copies:
+        copy.wait()
     await_piece(0)
     queries = project(lambda start: normed[:, start : start + depth], QUERY, local)
     stage(3)
@@ -452,24 +469,28 @@
                 * scale
             )
             raised = jnp.exp(scores - jnp.max(scores, axis=-1, keepdims=True))
-            probs = (raised / jnp.sum(raised, axis=-1, keepdims=True)).astype(bf16)
+            probs = (raised * (1.0 / jnp.sum(raised, axis=-1, keepdims=True))).astype(bf16)
             halves.append(jnp.dot(probs, pair_value, preferred_element_type=f32))
         attended[:, columns] = jnp.where(lane < HEAD_DIM, halves[0], halves[1]).astype(bf16)
 
     def merge(rows, unit, which):
+        copies = []
         for source in range(n_tm):
             term = jnp.dot(rows, weights[unit, source], preferred_element_type=f32)
             partial[which, :, :, source * depth : (source + 1) * depth] = term.astype(
                 bf16
             ).reshape(n_mp, block, local)
-        return swap(
-            "mp",
-            n_mp,
-            m,
-            which,
-            lambda peer: partial.at[which, peer],
-            gathered.at[which, m],
-        )
+            if source % 2 == 1:
+                columns = pl.ds((source - 1) * depth, 2 * depth)
+                copies += swap(
+                    "mp",
+                    n_mp,
+                    m,
+                    2 * which + source // 2,
+                    lambda peer: partial.at[which, peer, :, columns],
+                    gathered.at[which, m, :, columns],
+                )
+        return copies
 
     def merged(which):
         gathered[which, m] = partial[which, m]
@@ -482,8 +503,8 @@
     cross_copies = merge(attended[...], MERGE, 0)
     stage(4)
     finish(cross_copies)
-    gate_a = table[bucket_here, 2:3]
-    shift_b, scale_b = table[bucket_here, 3:4], table[bucket_here, 4:5]
+    gate_a = table[2, bucket_here, :]
+    shift_b, scale_b = table[3, bucket_here, :], table[4, bucket_here, :]
     middle[...] = latents[block_rows, :].astype(f32) + gate_a * merged(0)
     second[m] = (layer_norm(middle[...]) * (1.0 + scale_b) + shift_b).astype(bf16)
     share_start(second, 0)
@@ -506,8 +527,12 @@
         )
         if index < 2:
             stage(6 + index)
+    token = lax.broadcasted_iota(jnp.int32, (patch, tokens), 1)
+    first = lax.broadcasted_iota(jnp.int32, (patch, tokens), 0) + p * patch
+    picker = jnp.where(token == first, 1.0, 0.0).astype(bf16)
+    clear = jnp.where(clouds[...] == 0, 1.0, 0.0).astype(bf16)
+    seen = lax.dot_general(picker, clear, (((1,), (1,)), ((), ())), preferred_element_type=f32)
     finish(triple_copies)
-    seen = visible[pl.ds(pl.multiple_of(p * patch, 16), patch), :]
     time_key = across[:, 1].astype(f32)
     for date in range(n_tm):
         products = (across[date, 0].astype(f32)[None] * time_key).reshape(n_tm * patch, local)
@@ -524,10 +549,10 @@
         ]
         highest = functools.reduce(jnp.maximum, shown)
         raised = [jnp.exp(score - highest) for score in shown]
-        total = functools.reduce(jnp.add, raised)
+        inverse = 1.0 / functools.reduce(jnp.add, raised)
         result = None
         for other in range(n_tm):
-            prob = (raised[other] / total).astype(bf16).astype(f32)
+            prob = (raised[other] * inverse).astype(bf16).astype(f32)
             term = prob * across[other, 2].astype(f32)
             result = term if result is None else result + term
         mixed[date] = result.astype(bf16)
@@ -537,7 +562,7 @@
     await_piece(5)
     time_copies = merge(returned[...].reshape(tokens, local), TMERGE, 1)
     finish(time_copies)
-    gate_b = table[bucket_here, 5:6]
+    gate_b = table[5, bucket_here, :]
     updated[m] = (middle[...] + gate_b * merged(1)).astype(bf16)
     share_start(updated, 1)
     share_finish(updated, 1)
@@ -569,18 +594,7 @@
 ):
     tokens, width = latents.shape[2:]
     depth, local = cross_query.shape
-    shard = jnp.stack(
-        [
-            cross_query,
-            cross_merge,
-            time_triple[:, 0],
-            time_triple[:, 1],
-            time_triple[:, 2],
-            time_merge,
-        ]
-    )
     pair_shard = jnp.stack([cross_pairs[:, 0], cross_pairs[:, 1]])
-    visible = (clouds[0] == 0).astype(jnp.float32).T
     patch, block = tokens // n_tm, tokens // n_mp
     bf16, f32 = jnp.bfloat16, jnp.float32
     vmem = pl.BlockSpec(memory_space=pltpu.VMEM)
@@ -590,7 +604,7 @@
     result = pl.pallas_call(
         functools.partial(block_kernel, n_tm, n_mp),
         out_shape=jax.ShapeDtypeStruct((tokens, width), bf16),
-        in_specs=[vmem, vmem, smem, smem, vmem] + [pl.BlockSpec(memory_space=pl.ANY)] * 2,
+        in_specs=[vmem, vmem, smem, smem, vmem] + [pl.BlockSpec(memory_space=pl.ANY)] * 5,
         out_specs=vmem,
         scratch_shapes=[
             pltpu.VMEM((UNITS, n_tm, depth, local), bf16),
@@ -612,7 +626,7 @@
             pltpu.VMEM((n_tm, patch, local), bf16),
             pltpu.VMEM((n_mp, block, width), bf16),
             pltpu.VMEM((local, local), bf16),
-            dma,
+            dma((4,)),
             dma,
             dma((pieces, 2, n_tm - 1)),
             dma((pieces, 2, n_tm - 1)),
@@ -620,15 +634,26 @@
             dma((pieces, 2, n_tm - 1)),
             dma((7, n_tm - 1)),
             dma((7, n_tm - 1)),
-            dma((3, n_mp - 1)),
-            dma((3, n_mp - 1)),
+            dma((5, n_mp - 1)),
+            dma((5, n_mp - 1)),
             dma((2, PARTS, 3)),
             dma((2, PARTS, 3)),
         ],
         compiler_params=pltpu.CompilerParams(
             collective_id=0, has_side_effects=True, vmem_limit_bytes=56 * 1024 * 1024
         ),
-    )(latents[0, 0], gsd_table, gsd_bucket.reshape(1), clearest, visible, shard, pair_shard)
+    )(
+        latents[0, 0],
+        gsd_table.transpose(1, 0, 2),
+        gsd_bucket.reshape(1),
+        clearest,
+        clouds[0],
+        cross_query,
+        cross_merge,
+        time_triple.transpose(1, 0, 2),
+        time_merge,
+        pair_shard,
+    )
     return result[None, None]
 
 
@@ -640,7 +665,9 @@
         mesh.shape["group"] == 2
         and latents.shape[0] == 2
         and latents.shape[1] == n_tm
-        and n_tm <= 8
+        and n_tm in (2, 4, 8)
+        and tokens % 32 == 0
+        and (tokens // n_mp) % 32 == 0
         and n_mp == 4
         and tokens % (16 * n_tm) == 0
         and tokens % (16 * PARTS * n_mp) == 0

time: 129 us -> 123 us (0.953)
  local copies, waits for them, and re-layouts: 7.72 us -> 4.44 us
  other arithmetic: 2.25 us -> 0.88 us
    unnamed x15 -> x1, local copies, waits for them, and re-layouts: 6.58 us -> 2.06 us
    slice x1, local copies, waits for them, and re-layouts: 0.82 us -> 2.28 us  [fused(): pair_shard = jnp.stack([cross_pairs[:, 0], cross_pairs[:, 1]])]
where the time goes in v3:
time: 123 us
  Pallas kernels  117 us (95%)
  local copies, waits for them, and re-layouts  4.44 us (4%)
  between operations  1.32 us (1%)
    pallas_call x1, Pallas kernels, fused(): pl.pallas_call(functools.partial(block_kernel, n_tm, n_mp), out_shape=jax...  117 us

profile of v3, /device:TPU:0, one launch (start us, length us, event | category | flops | bytes accessed | tf_op | source)
XLA Modules:
  0.0 123.2 jit_solution(9252469698826578156)
XLA Ops:
  0.0 2.3 %fusion = (bf16[384,1,384]{2,1,0:T(2,128)(2,1)S(1)}, bf16[384,1,384]{2,1,0:T(2,128)(2,1)S(1)}) fusion(bf16[384,2,384]{2,1,0:T(2,128)(2,1)} %param.16), kind=kLoop, calls=%fused_computation.3 | loop fusion | bytes 1179648 | tf_op jit(solution)/shard_map/slice | solution.py:597
  2.3 0.1 copy_bitcast_fusion
  2.4 0.9 pad_maximum_fusion.pair_shard
  4.6 116.5 %shard_map.100 = bf16[256,1536]{1,0:T(8,128)(2,1)} custom-call(bf16[256,1536]{1,0:T(8,128)(2,1)} %bitcast.13, f32[6,8,1536]{2,1,0:T(8,128)} %bitcast.14, s32[1]{0:T(128)} %bitcast.10.bucket, s32[1]{0:T(128)S(6)} %copy.19.clearest, s32[4,256]{1,0:T(4,128)} %bitcast.15, bf16[384,384]{1,0:T(8,128)(2,1)} %query_shard.1, bf16[384,384]{1,0:T(8,128)(2,1)} %merge_shard.1, ...), custom_call_target="tpu_custom_call" | custom-call | tf_op jit(solution)/shard_map/pallas_call | solution.py:604
  121.1 2.1 %copy.20 = bf16[1,1,256,1536]{3,2,1,0:T(8,128)(2,1)} copy(bf16[1,1,256,1536]{3,2,1,0:T(8,128)(2,1)} %bitcast.11) | data formatting | bytes 1572864
